TPU v7x, 512 devices: a whole 4x8x8 slice. The times are simulated.
512 devices in a mesh: tm: 32 (over y, x), blk: 16 (over z, core).
Axes of the slice: x: 4, y: 8, z: 8, core: 2. Of those that a mesh axis runs over, the one named last changes fastest.
Arguments:
- panel_strip: bfloat16 [32, 8192, 2304], P('tm', 'blk'), may hold values from -6 to 6
- pivot_inverses: bfloat16 [32, 2, 256, 256], P('tm'), may hold values from -0.0234375 to 0.0234375
- coupling: float32 [32, 256, 256], P('tm'), may hold values from -0.375 to 0.375
- pivot_nodes: int32 [3, 256], replicated, may hold values from 0 to 8191, as said below
Outputs:
- trailing: bfloat16 [32, 8192, 1792], P('tm', 'blk')
- reduced: float32 [32, 256, 256], P('tm')
Inputs may be any that keep to these rules, and one draw needn't show every extreme that they name: `pivot_nodes`: entry j of every row is a node of the range [(j // 16) * 512, (j // 16 + 1) * 512); all 768 entries differ.
All inputs are finite; a program needn't handle non-finite values.
Results may differ from a plain program's by a relative error of at most 0.0068.
Values may be sent and summed in bfloat16 or wider, within the bound.
No kernel may reach another device: no remote copies, remote signals or barrier semaphores. Data moves between devices by JAX's collectives and lax.ppermute only.
A program may use at most 128 MiB of HBM per device.

v0:
```python
import jax
import jax.numpy as jnp
from jax import lax
from jax.sharding import PartitionSpec as P


def passed_along(x, axis, by):
    count = lax.axis_size(axis)
    pairs = [(i, i + by) for i in range(count) if 0 <= i + by < count]
    return lax.ppermute(x, axis, pairs)


def matmul_high(left, right):
    return jnp.dot(left, right, precision=lax.Precision.HIGHEST, preferred_element_type=jnp.float32)


def body(panel_strip, pivot_inverses, coupling, pivot_nodes):
    strip_block = panel_strip[0]
    inverse_pair = pivot_inverses[0]
    coupling_here = coupling[0]
    panel_width = inverse_pair.shape[-1]
    rows_here = strip_block.shape[0]
    blk_count = lax.axis_size("blk")
    per_device = panel_width // blk_count
    my_index = lax.axis_index("blk")
    local_rows = (
        lax.dynamic_slice_in_dim(pivot_nodes, my_index * per_device, per_device, 1)
        - my_index * rows_here
    )
    picker = (
        local_rows[:, :, None] == lax.broadcasted_iota(jnp.int32, (3, per_device, rows_here), 2)
    ).astype(jnp.bfloat16)
    factor_one = jnp.dot(
        strip_block[:, :panel_width], inverse_pair[0], preferred_element_type=jnp.float32
    ).astype(jnp.bfloat16)
    picked_one = jnp.dot(
        picker[0], strip_block[:, panel_width:], preferred_element_type=jnp.float32
    ).astype(jnp.bfloat16)
    columns = factor_one
    updated = (
        strip_block[:, panel_width:].astype(jnp.float32)
        - jnp.dot(
            columns,
            lax.all_gather(picked_one, "blk", axis=0, tiled=True),
            preferred_element_type=jnp.float32,
        )
    ).astype(jnp.bfloat16)
    factor_two = jnp.dot(
        updated[:, :panel_width], inverse_pair[1], preferred_element_type=jnp.float32
    ).astype(jnp.bfloat16)
    picked_two = jnp.dot(
        picker[1], updated[:, panel_width:], preferred_element_type=jnp.float32
    ).astype(jnp.bfloat16)
    columns = factor_two
    trailing = (
        updated[:, panel_width:].astype(jnp.float32)
        - jnp.dot(
            columns,
            lax.all_gather(picked_two, "blk", axis=0, tiled=True),
            preferred_element_type=jnp.float32,
        )
    ).astype(jnp.bfloat16)
    edge_rows = jnp.dot(
        picker[2], trailing[:, :panel_width], preferred_element_type=jnp.float32
    ).astype(jnp.bfloat16)
    boundary_block = lax.all_gather(edge_rows, "blk", axis=0, tiled=True).astype(jnp.float32)
    position = lax.axis_index("tm")

    def advance(turn_index, current):
        incoming = passed_along(current, "tm", 1)

        def apply_map(operand):
            return (
                matmul_high(matmul_high(coupling_here, operand), coupling_here.T) + boundary_block
            )

        def keep_state(operand):
            return current

        return lax.cond(position == turn_index, apply_map, keep_state, incoming)

    reduced = lax.fori_loop(1, lax.axis_size("tm"), advance, boundary_block)
    return (trailing[None], reduced[None])


def solution(mesh):
    placed = (P("tm", "blk", None), P("tm", None, None, None), P("tm", None, None), P())
    return jax.shard_map(
        body,
        mesh=mesh,
        in_specs=placed,
        out_specs=(P("tm", "blk", None), P("tm", None, None)),
        check_vma=False,
    )
```

profile of v0, /device:TPU:32, one launch (start us, length us, event | category | flops | bytes accessed | tf_op | source)
XLA Modules:
  0.0 484.5 jit_solution(10073837723274590851)
XLA Ops:
  10.7 46.4 %all-gather.2.cloned.1.call-done = bf16[256,2048]{1,0:T(8,128)(2,1)} async-done(((bf16[16,2048]{1,0:T(8,128)(2,1)}), bf16[256,2048]{1,0:T(8,128)(2,1)}) %all-gather.2.cloned.1.call-update) | async-done | bytes 1048592 | tf_op jit(solution)/shard_map/all_gather | solution.py:44
  60.3 18.0 %all_gather.10 = bf16[256,1792]{1,0:T(8,128)(2,1)S(1)} all-gather(bf16[16,1792]{1,0:T(8,128)(2,1)S(1)} %convolution_convert_fusion), channel_id=1, replica_groups=mesh['tm'=32,'blk'=16] {'blk'}, dimensions={0}, use_global_device_ids=true | all-gather | bytes 974848 | tf_op jit(solution)/shard_map/all_gather | solution.py:59
  82.4 15.1 %all_gather.11 = bf16[256,256]{1,0:T(8,128)(2,1)S(1)} all-gather(bf16[16,256]{1,0:T(8,128)(2,1)S(1)} %convolution_convert_fusion.4), channel_id=1, replica_groups=mesh['tm'=32,'blk'=16] {'blk'}, dimensions={0}, use_global_device_ids=true | all-gather | bytes 139264 | tf_op jit(solution)/shard_map/all_gather | solution.py:66
  97.6 379.3 %while.16 = (s32[]{:T(128)}, f32[256,256]{1,0:T(8,128)S(1)}, s32[]{:T(128)}, f32[256,256]{1,0:T(8,128)S(1)}, f32[256,256]{1,0:T(8,128)S(1)}, /*index=5*/s32[]{:T(128)}) while((s32[]{:T(128)}, f32[256,256]{1,0:T(8,128)S(1)}, s32[]{:T(128)}, f32[256,256]{1,0:T(8,128)S(1)}, f32[256,256]{1,0:T(8,128)S(1)}, /*index=5*/s32[]{:T(128)}) %tuple.51), condition=%wide.region_3.0_spmd, body=%wide.region_0.0_spmd.sunk | while | flops 402718720 | bytes 2883739 | solution.py:82
  101.0 10.4 %collective-permute-done = f32[256,256]{1,0:T(8,128)S(1)} collective-permute-done((f32[256,256]{1,0:T(8,128)S(1)}, f32[256,256]{1,0:T(8,128)S(1)}, u32[]{:S(2)}, u32[]{:S(2)}) %collective-permute-start) | collective-permute-done | bytes 262176 | tf_op jit(solution)/shard_map/while/body/eval_jaxpr/ppermute | solution.py:10
  113.3 11.0 %collective-permute-done = f32[256,256]{1,0:T(8,128)S(1)} collective-permute-done((f32[256,256]{1,0:T(8,128)S(1)}, f32[256,256]{1,0:T(8,128)S(1)}, u32[]{:S(2)}, u32[]{:S(2)}) %collective-permute-start) | collective-permute-done | bytes 262176 | tf_op jit(solution)/shard_map/while/body/eval_jaxpr/ppermute | solution.py:10
  126.3 10.1 %collective-permute-done = f32[256,256]{1,0:T(8,128)S(1)} collective-permute-done((f32[256,256]{1,0:T(8,128)S(1)}, f32[256,256]{1,0:T(8,128)S(1)}, u32[]{:S(2)}, u32[]{:S(2)}) %collective-permute-start) | collective-permute-done | bytes 262176 | tf_op jit(solution)/shard_map/while/body/eval_jaxpr/ppermute | solution.py:10
  173.0 9.7 %collective-permute-done = f32[256,256]{1,0:T(8,128)S(1)} collective-permute-done((f32[256,256]{1,0:T(8,128)S(1)}, f32[256,256]{1,0:T(8,128)S(1)}, u32[]{:S(2)}, u32[]{:S(2)}) %collective-permute-start) | collective-permute-done | bytes 262176 | tf_op jit(solution)/shard_map/while/body/eval_jaxpr/ppermute | solution.py:10
  184.6 9.8 %collective-permute-done = f32[256,256]{1,0:T(8,128)S(1)} collective-permute-done((f32[256,256]{1,0:T(8,128)S(1)}, f32[256,256]{1,0:T(8,128)S(1)}, u32[]{:S(2)}, u32[]{:S(2)}) %collective-permute-start) | collective-permute-done | bytes 262176 | tf_op jit(solution)/shard_map/while/body/eval_jaxpr/ppermute | solution.py:10
  196.3 10.9 %collective-permute-done = f32[256,256]{1,0:T(8,128)S(1)} collective-permute-done((f32[256,256]{1,0:T(8,128)S(1)}, f32[256,256]{1,0:T(8,128)S(1)}, u32[]{:S(2)}, u32[]{:S(2)}) %collective-permute-start) | collective-permute-done | bytes 262176 | tf_op jit(solution)/shard_map/while/body/eval_jaxpr/ppermute | solution.py:10
  209.2 12.1 %collective-permute-done = f32[256,256]{1,0:T(8,128)S(1)} collective-permute-done((f32[256,256]{1,0:T(8,128)S(1)}, f32[256,256]{1,0:T(8,128)S(1)}, u32[]{:S(2)}, u32[]{:S(2)}) %collective-permute-start) | collective-permute-done | bytes 262176 | tf_op jit(solution)/shard_map/while/body/eval_jaxpr/ppermute | solution.py:10
  223.3 11.6 %collective-permute-done = f32[256,256]{1,0:T(8,128)S(1)} collective-permute-done((f32[256,256]{1,0:T(8,128)S(1)}, f32[256,256]{1,0:T(8,128)S(1)}, u32[]{:S(2)}, u32[]{:S(2)}) %collective-permute-start) | collective-permute-done | bytes 262176 | tf_op jit(solution)/shard_map/while/body/eval_jaxpr/ppermute | solution.py:10
  236.8 10.8 %collective-permute-done = f32[256,256]{1,0:T(8,128)S(1)} collective-permute-done((f32[256,256]{1,0:T(8,128)S(1)}, f32[256,256]{1,0:T(8,128)S(1)}, u32[]{:S(2)}, u32[]{:S(2)}) %collective-permute-start) | collective-permute-done | bytes 262176 | tf_op jit(solution)/shard_map/while/body/eval_jaxpr/ppermute | solution.py:10
  249.5 9.9 %collective-permute-done = f32[256,256]{1,0:T(8,128)S(1)} collective-permute-done((f32[256,256]{1,0:T(8,128)S(1)}, f32[256,256]{1,0:T(8,128)S(1)}, u32[]{:S(2)}, u32[]{:S(2)}) %collective-permute-start) | collective-permute-done | bytes 262176 | tf_op jit(solution)/shard_map/while/body/eval_jaxpr/ppermute | solution.py:10
  284.5 9.7 %collective-permute-done = f32[256,256]{1,0:T(8,128)S(1)} collective-permute-done((f32[256,256]{1,0:T(8,128)S(1)}, f32[256,256]{1,0:T(8,128)S(1)}, u32[]{:S(2)}, u32[]{:S(2)}) %collective-permute-start) | collective-permute-done | bytes 262176 | tf_op jit(solution)/shard_map/while/body/eval_jaxpr/ppermute | solution.py:10
  296.9 9.7 %collective-permute-done = f32[256,256]{1,0:T(8,128)S(1)} collective-permute-done((f32[256,256]{1,0:T(8,128)S(1)}, f32[256,256]{1,0:T(8,128)S(1)}, u32[]{:S(2)}, u32[]{:S(2)}) %collective-permute-start) | collective-permute-done | bytes 262176 | tf_op jit(solution)/shard_map/while/body/eval_jaxpr/ppermute | solution.py:10
  308.4 10.1 %collective-permute-done = f32[256,256]{1,0:T(8,128)S(1)} collective-permute-done((f32[256,256]{1,0:T(8,128)S(1)}, f32[256,256]{1,0:T(8,128)S(1)}, u32[]{:S(2)}, u32[]{:S(2)}) %collective-permute-start) | collective-permute-done | bytes 262176 | tf_op jit(solution)/shard_map/while/body/eval_jaxpr/ppermute | solution.py:10
  320.4 11.2 %collective-permute-done = f32[256,256]{1,0:T(8,128)S(1)} collective-permute-done((f32[256,256]{1,0:T(8,128)S(1)}, f32[256,256]{1,0:T(8,128)S(1)}, u32[]{:S(2)}, u32[]{:S(2)}) %collective-permute-start) | collective-permute-done | bytes 262176 | tf_op jit(solution)/shard_map/while/body/eval_jaxpr/ppermute | solution.py:10
  333.6 12.3 %collective-permute-done = f32[256,256]{1,0:T(8,128)S(1)} collective-permute-done((f32[256,256]{1,0:T(8,128)S(1)}, f32[256,256]{1,0:T(8,128)S(1)}, u32[]{:S(2)}, u32[]{:S(2)}) %collective-permute-start) | collective-permute-done | bytes 262176 | tf_op jit(solution)/shard_map/while/body/eval_jaxpr/ppermute | solution.py:10
  347.8 11.6 %collective-permute-done = f32[256,256]{1,0:T(8,128)S(1)} collective-permute-done((f32[256,256]{1,0:T(8,128)S(1)}, f32[256,256]{1,0:T(8,128)S(1)}, u32[]{:S(2)}, u32[]{:S(2)}) %collective-permute-start) | collective-permute-done | bytes 262176 | tf_op jit(solution)/shard_map/while/body/eval_jaxpr/ppermute | solution.py:10
  361.3 10.8 %collective-permute-done = f32[256,256]{1,0:T(8,128)S(1)} collective-permute-done((f32[256,256]{1,0:T(8,128)S(1)}, f32[256,256]{1,0:T(8,128)S(1)}, u32[]{:S(2)}, u32[]{:S(2)}) %collective-permute-start) | collective-permute-done | bytes 262176 | tf_op jit(solution)/shard_map/while/body/eval_jaxpr/ppermute | solution.py:10
  374.0 9.8 %collective-permute-done = f32[256,256]{1,0:T(8,128)S(1)} collective-permute-done((f32[256,256]{1,0:T(8,128)S(1)}, f32[256,256]{1,0:T(8,128)S(1)}, u32[]{:S(2)}, u32[]{:S(2)}) %collective-permute-start) | collective-permute-done | bytes 262176 | tf_op jit(solution)/shard_map/while/body/eval_jaxpr/ppermute | solution.py:10
  409.0 9.7 %collective-permute-done = f32[256,256]{1,0:T(8,128)S(1)} collective-permute-done((f32[256,256]{1,0:T(8,128)S(1)}, f32[256,256]{1,0:T(8,128)S(1)}, u32[]{:S(2)}, u32[]{:S(2)}) %collective-permute-start) | collective-permute-done | bytes 262176 | tf_op jit(solution)/shard_map/while/body/eval_jaxpr/ppermute | solution.py:10
  432.1 10.1 %collective-permute-done = f32[256,256]{1,0:T(8,128)S(1)} collective-permute-done((f32[256,256]{1,0:T(8,128)S(1)}, f32[256,256]{1,0:T(8,128)S(1)}, u32[]{:S(2)}, u32[]{:S(2)}) %collective-permute-start) | collective-permute-done | bytes 262176 | tf_op jit(solution)/shard_map/while/body/eval_jaxpr/ppermute | solution.py:10
  (92 shorter events, 180.0 us)
Async XLA Ops:
  7.2 50.0 %all-gather.2.cloned.1.call-start = ((), (), s32[]{:S(2)}) async-start(), calls=%async_computation | async-start | bytes 1114112 | tf_op jit(solution)/shard_map/all_gather | solution.py:44
  97.6 13.8 %collective-permute-start = (f32[256,256]{1,0:T(8,128)S(1)}, f32[256,256]{1,0:T(8,128)S(1)}, u32[]{:S(2)}, u32[]{:S(2)}) collective-permute-start(f32[256,256]{1,0:T(8,128)S(1)} %get-tuple-element.162), channel_id=1, source_target_pairs={{0,16},{16,32},{32,48},{48,64},{64,80},{80,96},{96,112},{112,128},... | collective-permute-start | bytes 786440 | tf_op jit(solution)/shard_map/while/body/eval_jaxpr/ppermute | solution.py:10
  111.4 13.0 %collective-permute-start = (f32[256,256]{1,0:T(8,128)S(1)}, f32[256,256]{1,0:T(8,128)S(1)}, u32[]{:S(2)}, u32[]{:S(2)}) collective-permute-start(f32[256,256]{1,0:T(8,128)S(1)} %get-tuple-element.162), channel_id=1, source_target_pairs={{0,16},{16,32},{32,48},{48,64},{64,80},{80,96},{96,112},{112,128},... | collective-permute-start | bytes 786440 | tf_op jit(solution)/shard_map/while/body/eval_jaxpr/ppermute | solution.py:10
  124.3 12.0 %collective-permute-start = (f32[256,256]{1,0:T(8,128)S(1)}, f32[256,256]{1,0:T(8,128)S(1)}, u32[]{:S(2)}, u32[]{:S(2)}) collective-permute-start(f32[256,256]{1,0:T(8,128)S(1)} %get-tuple-element.162), channel_id=1, source_target_pairs={{0,16},{16,32},{32,48},{48,64},{64,80},{80,96},{96,112},{112,128},... | collective-permute-start | bytes 786440 | tf_op jit(solution)/shard_map/while/body/eval_jaxpr/ppermute | solution.py:10
  136.4 11.6 %collective-permute-start = (f32[256,256]{1,0:T(8,128)S(1)}, f32[256,256]{1,0:T(8,128)S(1)}, u32[]{:S(2)}, u32[]{:S(2)}) collective-permute-start(f32[256,256]{1,0:T(8,128)S(1)} %get-tuple-element.162), channel_id=1, source_target_pairs={{0,16},{16,32},{32,48},{48,64},{64,80},{80,96},{96,112},{112,128},... | collective-permute-start | bytes 786440 | tf_op jit(solution)/shard_map/while/body/eval_jaxpr/ppermute | solution.py:10
  147.9 11.6 %collective-permute-start = (f32[256,256]{1,0:T(8,128)S(1)}, f32[256,256]{1,0:T(8,128)S(1)}, u32[]{:S(2)}, u32[]{:S(2)}) collective-permute-start(f32[256,256]{1,0:T(8,128)S(1)} %get-tuple-element.162), channel_id=1, source_target_pairs={{0,16},{16,32},{32,48},{48,64},{64,80},{80,96},{96,112},{112,128},... | collective-permute-start | bytes 786440 | tf_op jit(solution)/shard_map/while/body/eval_jaxpr/ppermute | solution.py:10
  159.5 11.6 %collective-permute-start = (f32[256,256]{1,0:T(8,128)S(1)}, f32[256,256]{1,0:T(8,128)S(1)}, u32[]{:S(2)}, u32[]{:S(2)}) collective-permute-start(f32[256,256]{1,0:T(8,128)S(1)} %get-tuple-element.162), channel_id=1, source_target_pairs={{0,16},{16,32},{32,48},{48,64},{64,80},{80,96},{96,112},{112,128},... | collective-permute-start | bytes 786440 | tf_op jit(solution)/shard_map/while/body/eval_jaxpr/ppermute | solution.py:10
  171.1 11.6 %collective-permute-start = (f32[256,256]{1,0:T(8,128)S(1)}, f32[256,256]{1,0:T(8,128)S(1)}, u32[]{:S(2)}, u32[]{:S(2)}) collective-permute-start(f32[256,256]{1,0:T(8,128)S(1)} %get-tuple-element.162), channel_id=1, source_target_pairs={{0,16},{16,32},{32,48},{48,64},{64,80},{80,96},{96,112},{112,128},... | collective-permute-start | bytes 786440 | tf_op jit(solution)/shard_map/while/body/eval_jaxpr/ppermute | solution.py:10
  182.7 11.8 %collective-permute-start = (f32[256,256]{1,0:T(8,128)S(1)}, f32[256,256]{1,0:T(8,128)S(1)}, u32[]{:S(2)}, u32[]{:S(2)}) collective-permute-start(f32[256,256]{1,0:T(8,128)S(1)} %get-tuple-element.162), channel_id=1, source_target_pairs={{0,16},{16,32},{32,48},{48,64},{64,80},{80,96},{96,112},{112,128},... | collective-permute-start | bytes 786440 | tf_op jit(solution)/shard_map/while/body/eval_jaxpr/ppermute | solution.py:10
  194.4 12.8 %collective-permute-start = (f32[256,256]{1,0:T(8,128)S(1)}, f32[256,256]{1,0:T(8,128)S(1)}, u32[]{:S(2)}, u32[]{:S(2)}) collective-permute-start(f32[256,256]{1,0:T(8,128)S(1)} %get-tuple-element.162), channel_id=1, source_target_pairs={{0,16},{16,32},{32,48},{48,64},{64,80},{80,96},{96,112},{112,128},... | collective-permute-start | bytes 786440 | tf_op jit(solution)/shard_map/while/body/eval_jaxpr/ppermute | solution.py:10
  207.3 14.1 %collective-permute-start = (f32[256,256]{1,0:T(8,128)S(1)}, f32[256,256]{1,0:T(8,128)S(1)}, u32[]{:S(2)}, u32[]{:S(2)}) collective-permute-start(f32[256,256]{1,0:T(8,128)S(1)} %get-tuple-element.162), channel_id=1, source_target_pairs={{0,16},{16,32},{32,48},{48,64},{64,80},{80,96},{96,112},{112,128},... | collective-permute-start | bytes 786440 | tf_op jit(solution)/shard_map/while/body/eval_jaxpr/ppermute | solution.py:10
  221.3 13.5 %collective-permute-start = (f32[256,256]{1,0:T(8,128)S(1)}, f32[256,256]{1,0:T(8,128)S(1)}, u32[]{:S(2)}, u32[]{:S(2)}) collective-permute-start(f32[256,256]{1,0:T(8,128)S(1)} %get-tuple-element.162), channel_id=1, source_target_pairs={{0,16},{16,32},{32,48},{48,64},{64,80},{80,96},{96,112},{112,128},... | collective-permute-start | bytes 786440 | tf_op jit(solution)/shard_map/while/body/eval_jaxpr/ppermute | solution.py:10
  234.9 12.7 %collective-permute-start = (f32[256,256]{1,0:T(8,128)S(1)}, f32[256,256]{1,0:T(8,128)S(1)}, u32[]{:S(2)}, u32[]{:S(2)}) collective-permute-start(f32[256,256]{1,0:T(8,128)S(1)} %get-tuple-element.162), channel_id=1, source_target_pairs={{0,16},{16,32},{32,48},{48,64},{64,80},{80,96},{96,112},{112,128},... | collective-permute-start | bytes 786440 | tf_op jit(solution)/shard_map/while/body/eval_jaxpr/ppermute | solution.py:10
  247.6 11.8 %collective-permute-start = (f32[256,256]{1,0:T(8,128)S(1)}, f32[256,256]{1,0:T(8,128)S(1)}, u32[]{:S(2)}, u32[]{:S(2)}) collective-permute-start(f32[256,256]{1,0:T(8,128)S(1)} %get-tuple-element.162), channel_id=1, source_target_pairs={{0,16},{16,32},{32,48},{48,64},{64,80},{80,96},{96,112},{112,128},... | collective-permute-start | bytes 786440 | tf_op jit(solution)/shard_map/while/body/eval_jaxpr/ppermute | solution.py:10
  282.5 11.6 %collective-permute-start = (f32[256,256]{1,0:T(8,128)S(1)}, f32[256,256]{1,0:T(8,128)S(1)}, u32[]{:S(2)}, u32[]{:S(2)}) collective-permute-start(f32[256,256]{1,0:T(8,128)S(1)} %get-tuple-element.162), channel_id=1, source_target_pairs={{0,16},{16,32},{32,48},{48,64},{64,80},{80,96},{96,112},{112,128},... | collective-permute-start | bytes 786440 | tf_op jit(solution)/shard_map/while/body/eval_jaxpr/ppermute | solution.py:10
  294.9 11.6 %collective-permute-start = (f32[256,256]{1,0:T(8,128)S(1)}, f32[256,256]{1,0:T(8,128)S(1)}, u32[]{:S(2)}, u32[]{:S(2)}) collective-permute-start(f32[256,256]{1,0:T(8,128)S(1)} %get-tuple-element.162), channel_id=1, source_target_pairs={{0,16},{16,32},{32,48},{48,64},{64,80},{80,96},{96,112},{112,128},... | collective-permute-start | bytes 786440 | tf_op jit(solution)/shard_map/while/body/eval_jaxpr/ppermute | solution.py:10
  306.5 12.0 %collective-permute-start = (f32[256,256]{1,0:T(8,128)S(1)}, f32[256,256]{1,0:T(8,128)S(1)}, u32[]{:S(2)}, u32[]{:S(2)}) collective-permute-start(f32[256,256]{1,0:T(8,128)S(1)} %get-tuple-element.162), channel_id=1, source_target_pairs={{0,16},{16,32},{32,48},{48,64},{64,80},{80,96},{96,112},{112,128},... | collective-permute-start | bytes 786440 | tf_op jit(solution)/shard_map/while/body/eval_jaxpr/ppermute | solution.py:10
  318.5 13.1 %collective-permute-start = (f32[256,256]{1,0:T(8,128)S(1)}, f32[256,256]{1,0:T(8,128)S(1)}, u32[]{:S(2)}, u32[]{:S(2)}) collective-permute-start(f32[256,256]{1,0:T(8,128)S(1)} %get-tuple-element.162), channel_id=1, source_target_pairs={{0,16},{16,32},{32,48},{48,64},{64,80},{80,96},{96,112},{112,128},... | collective-permute-start | bytes 786440 | tf_op jit(solution)/shard_map/while/body/eval_jaxpr/ppermute | solution.py:10
  331.6 14.3 %collective-permute-start = (f32[256,256]{1,0:T(8,128)S(1)}, f32[256,256]{1,0:T(8,128)S(1)}, u32[]{:S(2)}, u32[]{:S(2)}) collective-permute-start(f32[256,256]{1,0:T(8,128)S(1)} %get-tuple-element.162), channel_id=1, source_target_pairs={{0,16},{16,32},{32,48},{48,64},{64,80},{80,96},{96,112},{112,128},... | collective-permute-start | bytes 786440 | tf_op jit(solution)/shard_map/while/body/eval_jaxpr/ppermute | solution.py:10
  345.9 13.5 %collective-permute-start = (f32[256,256]{1,0:T(8,128)S(1)}, f32[256,256]{1,0:T(8,128)S(1)}, u32[]{:S(2)}, u32[]{:S(2)}) collective-permute-start(f32[256,256]{1,0:T(8,128)S(1)} %get-tuple-element.162), channel_id=1, source_target_pairs={{0,16},{16,32},{32,48},{48,64},{64,80},{80,96},{96,112},{112,128},... | collective-permute-start | bytes 786440 | tf_op jit(solution)/shard_map/while/body/eval_jaxpr/ppermute | solution.py:10
  359.4 12.7 %collective-permute-start = (f32[256,256]{1,0:T(8,128)S(1)}, f32[256,256]{1,0:T(8,128)S(1)}, u32[]{:S(2)}, u32[]{:S(2)}) collective-permute-start(f32[256,256]{1,0:T(8,128)S(1)} %get-tuple-element.162), channel_id=1, source_target_pairs={{0,16},{16,32},{32,48},{48,64},{64,80},{80,96},{96,112},{112,128},... | collective-permute-start | bytes 786440 | tf_op jit(solution)/shard_map/while/body/eval_jaxpr/ppermute | solution.py:10
  372.1 11.8 %collective-permute-start = (f32[256,256]{1,0:T(8,128)S(1)}, f32[256,256]{1,0:T(8,128)S(1)}, u32[]{:S(2)}, u32[]{:S(2)}) collective-permute-start(f32[256,256]{1,0:T(8,128)S(1)} %get-tuple-element.162), channel_id=1, source_target_pairs={{0,16},{16,32},{32,48},{48,64},{64,80},{80,96},{96,112},{112,128},... | collective-permute-start | bytes 786440 | tf_op jit(solution)/shard_map/while/body/eval_jaxpr/ppermute | solution.py:10
  407.0 11.6 %collective-permute-start = (f32[256,256]{1,0:T(8,128)S(1)}, f32[256,256]{1,0:T(8,128)S(1)}, u32[]{:S(2)}, u32[]{:S(2)}) collective-permute-start(f32[256,256]{1,0:T(8,128)S(1)} %get-tuple-element.162), channel_id=1, source_target_pairs={{0,16},{16,32},{32,48},{48,64},{64,80},{80,96},{96,112},{112,128},... | collective-permute-start | bytes 786440 | tf_op jit(solution)/shard_map/while/body/eval_jaxpr/ppermute | solution.py:10
  430.2 12.0 %collective-permute-start = (f32[256,256]{1,0:T(8,128)S(1)}, f32[256,256]{1,0:T(8,128)S(1)}, u32[]{:S(2)}, u32[]{:S(2)}) collective-permute-start(f32[256,256]{1,0:T(8,128)S(1)} %get-tuple-element.162), channel_id=1, source_target_pairs={{0,16},{16,32},{32,48},{48,64},{64,80},{80,96},{96,112},{112,128},... | collective-permute-start | bytes 786440 | tf_op jit(solution)/shard_map/while/body/eval_jaxpr/ppermute | solution.py:10
  (11 other events, 162.6 us)
Sparse Core Ops, SparseCore 0:
  10.9 46.2 all-gather.1
where the time goes:
time: 486 us; the launch traced here: 484 us
  waiting for transfers between devices  364 us (75%)
  starting transfers between devices  60.7 us (12%)
  blocking collectives  33.1 us (7%)
  between operations  14.1 us (3%)
  matrix products  10.7 us (2%)
    ppermute x31, waiting for transfers between devices, passed_along(): return lax.ppermute(x, axis, pairs)  317 us
    ppermute x31, starting transfers between devices, passed_along(): return lax.ppermute(x, axis, pairs)  60.6 us
    all_gather x1, waiting for transfers between devices, body(): lax.all_gather(picked_one, 'blk', axis=0, tiled=True)  46.4 us
    all_gather x1, blocking collectives, body(): lax.all_gather(picked_two, 'blk', axis=0, tiled=True)  18 us
    all_gather x1, blocking collectives, body(): lax.all_gather(edge_rows, 'blk', axis=0, tiled=True).astype(jnp.float32)  15.1 us
  transfers between devices with their start and end apart: 32, of which 32 were waited for; matrix products, arithmetic and copies ran while one was open for 0% of the time, Pallas kernels for 0%

commit v1 on v0

--- a/solution.py
+++ b/solution.py
@@ -1,7 +1,36 @@
+import functools
 import jax
 import jax.numpy as jnp
 from jax import lax
 from jax.sharding import PartitionSpec as P
+
+
+def test_zones_by_axis(v0, comm_axis):
+    local_part = lax.axis_size(comm_axis)
+    right_arr = lax.axis_index(comm_axis)
+    main, s_next, y2 = (local_part, right_arr, v0.shape[0])
+    ledger = [pp * main if p == 0 else pp for p, pp in enumerate(v0.shape)]
+    arr_out = jnp.zeros(ledger, v0.dtype)
+    carry_out = lax.dynamic_update_slice_in_dim(arr_out, v0, s_next * y2, axis=0)
+    near = w2 = v0
+    dev = 1
+    while dev < main // 2 + 1:
+        near = lax.ppermute(near, comm_axis, [(p, (p + 1) % main) for p in range(main)])
+        carry_out = lax.dynamic_update_slice_in_dim(
+            carry_out, near, (s_next - dev) % main * y2, axis=0
+        )
+        if 2 * dev < main:
+            w2 = lax.ppermute(
+                w2, axis_name=comm_axis, perm=[(p, (p - 1) % main) for p in range(main)]
+            )
+            carry_out = lax.dynamic_update_slice_in_dim(
+                carry_out, w2, (s_next + dev) % main * y2, axis=0
+            )
+        dev += 1
+    return carry_out
+
+
+treat_rounds_now = functools.partial(test_zones_by_axis, comm_axis="blk")
 
 
 def passed_along(x, axis, by):
@@ -54,11 +83,7 @@
     columns = factor_two
     trailing = (
         updated[:, panel_width:].astype(jnp.float32)
-        - jnp.dot(
-            columns,
-            lax.all_gather(picked_two, "blk", axis=0, tiled=True),
-            preferred_element_type=jnp.float32,
-        )
+        - jnp.dot(columns, treat_rounds_now(picked_two), preferred_element_type=jnp.float32)
     ).astype(jnp.bfloat16)
     edge_rows = jnp.dot(
         picker[2], trailing[:, :panel_width], preferred_element_type=jnp.float32

time: 486 us -> 506 us (1.041)
  starting transfers between devices: 60.7 us -> 81.4 us
  blocking collectives: 33.1 us -> 14.5 us
  waiting for transfers between devices: 364 us -> 381 us
    ppermute x0 -> x15, starting transfers between devices: none -> 20.7 us  [the longest x7 20.4 us: test_zones_by_axis(): lax.ppermute(w2, axis_name=comm_axis, perm=[(p, (p - 1) % main) for p in...]
    all_gather x1 -> x0, blocking collectives: 18 us -> none  [body(): lax.all_gather(picked_two, 'blk', axis=0, tiled=True)]
    ppermute x0 -> x15, waiting for transfers between devices: none -> 17.6 us  [the longest x8 17.6 us: test_zones_by_axis(): lax.ppermute(near, comm_axis, [(p, (p + 1) % main) for p in range(main)])]
  transfers between devices with their start and end apart: 32 -> 47, of which waited for: 32 -> 40; matrix products, arithmetic and copies ran while one was open for 0% -> 0% of each run, Pallas kernels for 0% -> 0%
where the time goes in v1:
time: 506 us; the launch traced here: 504 us
  waiting for transfers between devices  381 us (75%)
  starting transfers between devices  81.4 us (16%)
  blocking collectives  14.5 us (3%)
  between operations  14.2 us (3%)
  matrix products  10.7 us (2%)
    ppermute x31, waiting for transfers between devices, passed_along(): return lax.ppermute(x, axis, pairs)  317 us
    ppermute x31, starting transfers between devices, passed_along(): return lax.ppermute(x, axis, pairs)  60.6 us
    all_gather x1, waiting for transfers between devices, body(): lax.all_gather(picked_one, 'blk', axis=0, tiled=True)  46.4 us
    ppermute x7, starting transfers between devices, test_zones_by_axis(): lax.ppermute(w2, axis_name=comm_axis, perm=[(p, (p - 1) % main) for p in...  20.4 us
    ppermute x8, waiting for transfers between devices, test_zones_by_axis(): lax.ppermute(near, comm_axis, [(p, (p + 1) % main) for p in range(main)])  17.6 us
    all_gather x1, blocking collectives, body(): lax.all_gather(edge_rows, 'blk', axis=0, tiled=True).astype(jnp.float32)  14.5 us
  transfers between devices with their start and end apart: 47, of which 40 were waited for; matrix products, arithmetic and copies ran while one was open for 0% of the time, Pallas kernels for 0%

profile of v1, /device:TPU:32, one launch (start us, length us, event | category | flops | bytes accessed | tf_op | source)
XLA Modules:
  0.0 504.5 jit_solution(7437881353997894525)
XLA Ops:
  10.7 46.4 %all-gather.2.cloned.1.call-done = bf16[256,2048]{1,0:T(8,128)(2,1)} async-done(((bf16[16,2048]{1,0:T(8,128)(2,1)}), bf16[256,2048]{1,0:T(8,128)(2,1)}) %all-gather.2.cloned.1.call-update) | async-done | bytes 1048592 | tf_op jit(solution)/shard_map/all_gather | solution.py:73
  103.1 14.5 %all_gather.7 = bf16[256,256]{1,0:T(8,128)(2,1)S(1)} all-gather(bf16[16,256]{1,0:T(8,128)(2,1)S(1)} %convolution_convert_fusion.4), channel_id=1, replica_groups=mesh['tm'=32,'blk'=16] {'blk'}, dimensions={0}, use_global_device_ids=true | all-gather | bytes 139264 | tf_op jit(solution)/shard_map/all_gather | solution.py:91
  117.6 379.3 %while.16 = (s32[]{:T(128)}, f32[256,256]{1,0:T(8,128)S(1)}, s32[]{:T(128)}, f32[256,256]{1,0:T(8,128)S(1)}, f32[256,256]{1,0:T(8,128)S(1)}, /*index=5*/s32[]{:T(128)}) while((s32[]{:T(128)}, f32[256,256]{1,0:T(8,128)S(1)}, s32[]{:T(128)}, f32[256,256]{1,0:T(8,128)S(1)}, f32[256,256]{1,0:T(8,128)S(1)}, /*index=5*/s32[]{:T(128)}) %tuple.52), condition=%wide.region_3.4_spmd, body=%wide.region_0.3_spmd.sunk | while | flops 402718720 | bytes 2883739 | solution.py:107
  121.0 10.4 %collective-permute-done = f32[256,256]{1,0:T(8,128)S(1)} collective-permute-done((f32[256,256]{1,0:T(8,128)S(1)}, f32[256,256]{1,0:T(8,128)S(1)}, u32[]{:S(2)}, u32[]{:S(2)}) %collective-permute-start) | collective-permute-done | bytes 262176 | tf_op jit(solution)/shard_map/while/body/eval_jaxpr/ppermute | solution.py:39
  133.3 11.0 %collective-permute-done = f32[256,256]{1,0:T(8,128)S(1)} collective-permute-done((f32[256,256]{1,0:T(8,128)S(1)}, f32[256,256]{1,0:T(8,128)S(1)}, u32[]{:S(2)}, u32[]{:S(2)}) %collective-permute-start) | collective-permute-done | bytes 262176 | tf_op jit(solution)/shard_map/while/body/eval_jaxpr/ppermute | solution.py:39
  146.3 10.1 %collective-permute-done = f32[256,256]{1,0:T(8,128)S(1)} collective-permute-done((f32[256,256]{1,0:T(8,128)S(1)}, f32[256,256]{1,0:T(8,128)S(1)}, u32[]{:S(2)}, u32[]{:S(2)}) %collective-permute-start) | collective-permute-done | bytes 262176 | tf_op jit(solution)/shard_map/while/body/eval_jaxpr/ppermute | solution.py:39
  158.3 9.7 %collective-permute-done = f32[256,256]{1,0:T(8,128)S(1)} collective-permute-done((f32[256,256]{1,0:T(8,128)S(1)}, f32[256,256]{1,0:T(8,128)S(1)}, u32[]{:S(2)}, u32[]{:S(2)}) %collective-permute-start) | collective-permute-done | bytes 262176 | tf_op jit(solution)/shard_map/while/body/eval_jaxpr/ppermute | solution.py:39
  169.9 9.7 %collective-permute-done = f32[256,256]{1,0:T(8,128)S(1)} collective-permute-done((f32[256,256]{1,0:T(8,128)S(1)}, f32[256,256]{1,0:T(8,128)S(1)}, u32[]{:S(2)}, u32[]{:S(2)}) %collective-permute-start) | collective-permute-done | bytes 262176 | tf_op jit(solution)/shard_map/while/body/eval_jaxpr/ppermute | solution.py:39
  181.5 9.7 %collective-permute-done = f32[256,256]{1,0:T(8,128)S(1)} collective-permute-done((f32[256,256]{1,0:T(8,128)S(1)}, f32[256,256]{1,0:T(8,128)S(1)}, u32[]{:S(2)}, u32[]{:S(2)}) %collective-permute-start) | collective-permute-done | bytes 262176 | tf_op jit(solution)/shard_map/while/body/eval_jaxpr/ppermute | solution.py:39
  204.6 9.8 %collective-permute-done = f32[256,256]{1,0:T(8,128)S(1)} collective-permute-done((f32[256,256]{1,0:T(8,128)S(1)}, f32[256,256]{1,0:T(8,128)S(1)}, u32[]{:S(2)}, u32[]{:S(2)}) %collective-permute-start) | collective-permute-done | bytes 262176 | tf_op jit(solution)/shard_map/while/body/eval_jaxpr/ppermute | solution.py:39
  216.4 10.9 %collective-permute-done = f32[256,256]{1,0:T(8,128)S(1)} collective-permute-done((f32[256,256]{1,0:T(8,128)S(1)}, f32[256,256]{1,0:T(8,128)S(1)}, u32[]{:S(2)}, u32[]{:S(2)}) %collective-permute-start) | collective-permute-done | bytes 262176 | tf_op jit(solution)/shard_map/while/body/eval_jaxpr/ppermute | solution.py:39
  229.2 12.1 %collective-permute-done = f32[256,256]{1,0:T(8,128)S(1)} collective-permute-done((f32[256,256]{1,0:T(8,128)S(1)}, f32[256,256]{1,0:T(8,128)S(1)}, u32[]{:S(2)}, u32[]{:S(2)}) %collective-permute-start) | collective-permute-done | bytes 262176 | tf_op jit(solution)/shard_map/while/body/eval_jaxpr/ppermute | solution.py:39
  243.3 11.6 %collective-permute-done = f32[256,256]{1,0:T(8,128)S(1)} collective-permute-done((f32[256,256]{1,0:T(8,128)S(1)}, f32[256,256]{1,0:T(8,128)S(1)}, u32[]{:S(2)}, u32[]{:S(2)}) %collective-permute-start) | collective-permute-done | bytes 262176 | tf_op jit(solution)/shard_map/while/body/eval_jaxpr/ppermute | solution.py:39
  256.8 10.8 %collective-permute-done = f32[256,256]{1,0:T(8,128)S(1)} collective-permute-done((f32[256,256]{1,0:T(8,128)S(1)}, f32[256,256]{1,0:T(8,128)S(1)}, u32[]{:S(2)}, u32[]{:S(2)}) %collective-permute-start) | collective-permute-done | bytes 262176 | tf_op jit(solution)/shard_map/while/body/eval_jaxpr/ppermute | solution.py:39
  269.5 9.9 %collective-permute-done = f32[256,256]{1,0:T(8,128)S(1)} collective-permute-done((f32[256,256]{1,0:T(8,128)S(1)}, f32[256,256]{1,0:T(8,128)S(1)}, u32[]{:S(2)}, u32[]{:S(2)}) %collective-permute-start) | collective-permute-done | bytes 262176 | tf_op jit(solution)/shard_map/while/body/eval_jaxpr/ppermute | solution.py:39
  281.3 9.7 %collective-permute-done = f32[256,256]{1,0:T(8,128)S(1)} collective-permute-done((f32[256,256]{1,0:T(8,128)S(1)}, f32[256,256]{1,0:T(8,128)S(1)}, u32[]{:S(2)}, u32[]{:S(2)}) %collective-permute-start) | collective-permute-done | bytes 262176 | tf_op jit(solution)/shard_map/while/body/eval_jaxpr/ppermute | solution.py:39
  292.9 9.7 %collective-permute-done = f32[256,256]{1,0:T(8,128)S(1)} collective-permute-done((f32[256,256]{1,0:T(8,128)S(1)}, f32[256,256]{1,0:T(8,128)S(1)}, u32[]{:S(2)}, u32[]{:S(2)}) %collective-permute-start) | collective-permute-done | bytes 262176 | tf_op jit(solution)/shard_map/while/body/eval_jaxpr/ppermute | solution.py:39
  328.5 10.1 %collective-permute-done = f32[256,256]{1,0:T(8,128)S(1)} collective-permute-done((f32[256,256]{1,0:T(8,128)S(1)}, f32[256,256]{1,0:T(8,128)S(1)}, u32[]{:S(2)}, u32[]{:S(2)}) %collective-permute-start) | collective-permute-done | bytes 262176 | tf_op jit(solution)/shard_map/while/body/eval_jaxpr/ppermute | solution.py:39
  340.5 11.2 %collective-permute-done = f32[256,256]{1,0:T(8,128)S(1)} collective-permute-done((f32[256,256]{1,0:T(8,128)S(1)}, f32[256,256]{1,0:T(8,128)S(1)}, u32[]{:S(2)}, u32[]{:S(2)}) %collective-permute-start) | collective-permute-done | bytes 262176 | tf_op jit(solution)/shard_map/while/body/eval_jaxpr/ppermute | solution.py:39
  353.6 12.3 %collective-permute-done = f32[256,256]{1,0:T(8,128)S(1)} collective-permute-done((f32[256,256]{1,0:T(8,128)S(1)}, f32[256,256]{1,0:T(8,128)S(1)}, u32[]{:S(2)}, u32[]{:S(2)}) %collective-permute-start) | collective-permute-done | bytes 262176 | tf_op jit(solution)/shard_map/while/body/eval_jaxpr/ppermute | solution.py:39
  367.8 11.6 %collective-permute-done = f32[256,256]{1,0:T(8,128)S(1)} collective-permute-done((f32[256,256]{1,0:T(8,128)S(1)}, f32[256,256]{1,0:T(8,128)S(1)}, u32[]{:S(2)}, u32[]{:S(2)}) %collective-permute-start) | collective-permute-done | bytes 262176 | tf_op jit(solution)/shard_map/while/body/eval_jaxpr/ppermute | solution.py:39
  381.4 10.8 %collective-permute-done = f32[256,256]{1,0:T(8,128)S(1)} collective-permute-done((f32[256,256]{1,0:T(8,128)S(1)}, f32[256,256]{1,0:T(8,128)S(1)}, u32[]{:S(2)}, u32[]{:S(2)}) %collective-permute-start) | collective-permute-done | bytes 262176 | tf_op jit(solution)/shard_map/while/body/eval_jaxpr/ppermute | solution.py:39
  394.1 9.8 %collective-permute-done = f32[256,256]{1,0:T(8,128)S(1)} collective-permute-done((f32[256,256]{1,0:T(8,128)S(1)}, f32[256,256]{1,0:T(8,128)S(1)}, u32[]{:S(2)}, u32[]{:S(2)}) %collective-permute-start) | collective-permute-done | bytes 262176 | tf_op jit(solution)/shard_map/while/body/eval_jaxpr/ppermute | solution.py:39
  452.1 10.1 %collective-permute-done = f32[256,256]{1,0:T(8,128)S(1)} collective-permute-done((f32[256,256]{1,0:T(8,128)S(1)}, f32[256,256]{1,0:T(8,128)S(1)}, u32[]{:S(2)}, u32[]{:S(2)}) %collective-permute-start) | collective-permute-done | bytes 262176 | tf_op jit(solution)/shard_map/while/body/eval_jaxpr/ppermute | solution.py:39
  (137 shorter events, 208.9 us)
Async XLA Ops:
  7.2 50.0 %all-gather.2.cloned.1.call-start = ((), (), s32[]{:S(2)}) async-start(), calls=%async_computation | async-start | bytes 1114112 | tf_op jit(solution)/shard_map/all_gather | solution.py:73
  117.6 13.8 %collective-permute-start = (f32[256,256]{1,0:T(8,128)S(1)}, f32[256,256]{1,0:T(8,128)S(1)}, u32[]{:S(2)}, u32[]{:S(2)}) collective-permute-start(f32[256,256]{1,0:T(8,128)S(1)} %get-tuple-element.164), channel_id=1, source_target_pairs={{0,16},{16,32},{32,48},{48,64},{64,80},{80,96},{96,112},{112,128},... | collective-permute-start | bytes 786440 | tf_op jit(solution)/shard_map/while/body/eval_jaxpr/ppermute | solution.py:39
  131.4 13.0 %collective-permute-start = (f32[256,256]{1,0:T(8,128)S(1)}, f32[256,256]{1,0:T(8,128)S(1)}, u32[]{:S(2)}, u32[]{:S(2)}) collective-permute-start(f32[256,256]{1,0:T(8,128)S(1)} %get-tuple-element.164), channel_id=1, source_target_pairs={{0,16},{16,32},{32,48},{48,64},{64,80},{80,96},{96,112},{112,128},... | collective-permute-start | bytes 786440 | tf_op jit(solution)/shard_map/while/body/eval_jaxpr/ppermute | solution.py:39
  144.3 12.0 %collective-permute-start = (f32[256,256]{1,0:T(8,128)S(1)}, f32[256,256]{1,0:T(8,128)S(1)}, u32[]{:S(2)}, u32[]{:S(2)}) collective-permute-start(f32[256,256]{1,0:T(8,128)S(1)} %get-tuple-element.164), channel_id=1, source_target_pairs={{0,16},{16,32},{32,48},{48,64},{64,80},{80,96},{96,112},{112,128},... | collective-permute-start | bytes 786440 | tf_op jit(solution)/shard_map/while/body/eval_jaxpr/ppermute | solution.py:39
  156.4 11.6 %collective-permute-start = (f32[256,256]{1,0:T(8,128)S(1)}, f32[256,256]{1,0:T(8,128)S(1)}, u32[]{:S(2)}, u32[]{:S(2)}) collective-permute-start(f32[256,256]{1,0:T(8,128)S(1)} %get-tuple-element.164), channel_id=1, source_target_pairs={{0,16},{16,32},{32,48},{48,64},{64,80},{80,96},{96,112},{112,128},... | collective-permute-start | bytes 786440 | tf_op jit(solution)/shard_map/while/body/eval_jaxpr/ppermute | solution.py:39
  168.0 11.6 %collective-permute-start = (f32[256,256]{1,0:T(8,128)S(1)}, f32[256,256]{1,0:T(8,128)S(1)}, u32[]{:S(2)}, u32[]{:S(2)}) collective-permute-start(f32[256,256]{1,0:T(8,128)S(1)} %get-tuple-element.164), channel_id=1, source_target_pairs={{0,16},{16,32},{32,48},{48,64},{64,80},{80,96},{96,112},{112,128},... | collective-permute-start | bytes 786440 | tf_op jit(solution)/shard_map/while/body/eval_jaxpr/ppermute | solution.py:39
  179.5 11.6 %collective-permute-start = (f32[256,256]{1,0:T(8,128)S(1)}, f32[256,256]{1,0:T(8,128)S(1)}, u32[]{:S(2)}, u32[]{:S(2)}) collective-permute-start(f32[256,256]{1,0:T(8,128)S(1)} %get-tuple-element.164), channel_id=1, source_target_pairs={{0,16},{16,32},{32,48},{48,64},{64,80},{80,96},{96,112},{112,128},... | collective-permute-start | bytes 786440 | tf_op jit(solution)/shard_map/while/body/eval_jaxpr/ppermute | solution.py:39
  191.1 11.6 %collective-permute-start = (f32[256,256]{1,0:T(8,128)S(1)}, f32[256,256]{1,0:T(8,128)S(1)}, u32[]{:S(2)}, u32[]{:S(2)}) collective-permute-start(f32[256,256]{1,0:T(8,128)S(1)} %get-tuple-element.164), channel_id=1, source_target_pairs={{0,16},{16,32},{32,48},{48,64},{64,80},{80,96},{96,112},{112,128},... | collective-permute-start | bytes 786440 | tf_op jit(solution)/shard_map/while/body/eval_jaxpr/ppermute | solution.py:39
  202.7 11.8 %collective-permute-start = (f32[256,256]{1,0:T(8,128)S(1)}, f32[256,256]{1,0:T(8,128)S(1)}, u32[]{:S(2)}, u32[]{:S(2)}) collective-permute-start(f32[256,256]{1,0:T(8,128)S(1)} %get-tuple-element.164), channel_id=1, source_target_pairs={{0,16},{16,32},{32,48},{48,64},{64,80},{80,96},{96,112},{112,128},... | collective-permute-start | bytes 786440 | tf_op jit(solution)/shard_map/while/body/eval_jaxpr/ppermute | solution.py:39
  214.4 12.8 %collective-permute-start = (f32[256,256]{1,0:T(8,128)S(1)}, f32[256,256]{1,0:T(8,128)S(1)}, u32[]{:S(2)}, u32[]{:S(2)}) collective-permute-start(f32[256,256]{1,0:T(8,128)S(1)} %get-tuple-element.164), channel_id=1, source_target_pairs={{0,16},{16,32},{32,48},{48,64},{64,80},{80,96},{96,112},{112,128},... | collective-permute-start | bytes 786440 | tf_op jit(solution)/shard_map/while/body/eval_jaxpr/ppermute | solution.py:39
  227.3 14.1 %collective-permute-start = (f32[256,256]{1,0:T(8,128)S(1)}, f32[256,256]{1,0:T(8,128)S(1)}, u32[]{:S(2)}, u32[]{:S(2)}) collective-permute-start(f32[256,256]{1,0:T(8,128)S(1)} %get-tuple-element.164), channel_id=1, source_target_pairs={{0,16},{16,32},{32,48},{48,64},{64,80},{80,96},{96,112},{112,128},... | collective-permute-start | bytes 786440 | tf_op jit(solution)/shard_map/while/body/eval_jaxpr/ppermute | solution.py:39
  241.3 13.5 %collective-permute-start = (f32[256,256]{1,0:T(8,128)S(1)}, f32[256,256]{1,0:T(8,128)S(1)}, u32[]{:S(2)}, u32[]{:S(2)}) collective-permute-start(f32[256,256]{1,0:T(8,128)S(1)} %get-tuple-element.164), channel_id=1, source_target_pairs={{0,16},{16,32},{32,48},{48,64},{64,80},{80,96},{96,112},{112,128},... | collective-permute-start | bytes 786440 | tf_op jit(solution)/shard_map/while/body/eval_jaxpr/ppermute | solution.py:39
  254.9 12.7 %collective-permute-start = (f32[256,256]{1,0:T(8,128)S(1)}, f32[256,256]{1,0:T(8,128)S(1)}, u32[]{:S(2)}, u32[]{:S(2)}) collective-permute-start(f32[256,256]{1,0:T(8,128)S(1)} %get-tuple-element.164), channel_id=1, source_target_pairs={{0,16},{16,32},{32,48},{48,64},{64,80},{80,96},{96,112},{112,128},... | collective-permute-start | bytes 786440 | tf_op jit(solution)/shard_map/while/body/eval_jaxpr/ppermute | solution.py:39
  267.6 11.8 %collective-permute-start = (f32[256,256]{1,0:T(8,128)S(1)}, f32[256,256]{1,0:T(8,128)S(1)}, u32[]{:S(2)}, u32[]{:S(2)}) collective-permute-start(f32[256,256]{1,0:T(8,128)S(1)} %get-tuple-element.164), channel_id=1, source_target_pairs={{0,16},{16,32},{32,48},{48,64},{64,80},{80,96},{96,112},{112,128},... | collective-permute-start | bytes 786440 | tf_op jit(solution)/shard_map/while/body/eval_jaxpr/ppermute | solution.py:39
  314.9 11.6 %collective-permute-start = (f32[256,256]{1,0:T(8,128)S(1)}, f32[256,256]{1,0:T(8,128)S(1)}, u32[]{:S(2)}, u32[]{:S(2)}) collective-permute-start(f32[256,256]{1,0:T(8,128)S(1)} %get-tuple-element.164), channel_id=1, source_target_pairs={{0,16},{16,32},{32,48},{48,64},{64,80},{80,96},{96,112},{112,128},... | collective-permute-start | bytes 786440 | tf_op jit(solution)/shard_map/while/body/eval_jaxpr/ppermute | solution.py:39
  326.5 12.0 %collective-permute-start = (f32[256,256]{1,0:T(8,128)S(1)}, f32[256,256]{1,0:T(8,128)S(1)}, u32[]{:S(2)}, u32[]{:S(2)}) collective-permute-start(f32[256,256]{1,0:T(8,128)S(1)} %get-tuple-element.164), channel_id=1, source_target_pairs={{0,16},{16,32},{32,48},{48,64},{64,80},{80,96},{96,112},{112,128},... | collective-permute-start | bytes 786440 | tf_op jit(solution)/shard_map/while/body/eval_jaxpr/ppermute | solution.py:39
  338.5 13.1 %collective-permute-start = (f32[256,256]{1,0:T(8,128)S(1)}, f32[256,256]{1,0:T(8,128)S(1)}, u32[]{:S(2)}, u32[]{:S(2)}) collective-permute-start(f32[256,256]{1,0:T(8,128)S(1)} %get-tuple-element.164), channel_id=1, source_target_pairs={{0,16},{16,32},{32,48},{48,64},{64,80},{80,96},{96,112},{112,128},... | collective-permute-start | bytes 786440 | tf_op jit(solution)/shard_map/while/body/eval_jaxpr/ppermute | solution.py:39
  351.6 14.3 %collective-permute-start = (f32[256,256]{1,0:T(8,128)S(1)}, f32[256,256]{1,0:T(8,128)S(1)}, u32[]{:S(2)}, u32[]{:S(2)}) collective-permute-start(f32[256,256]{1,0:T(8,128)S(1)} %get-tuple-element.164), channel_id=1, source_target_pairs={{0,16},{16,32},{32,48},{48,64},{64,80},{80,96},{96,112},{112,128},... | collective-permute-start | bytes 786440 | tf_op jit(solution)/shard_map/while/body/eval_jaxpr/ppermute | solution.py:39
  365.9 13.5 %collective-permute-start = (f32[256,256]{1,0:T(8,128)S(1)}, f32[256,256]{1,0:T(8,128)S(1)}, u32[]{:S(2)}, u32[]{:S(2)}) collective-permute-start(f32[256,256]{1,0:T(8,128)S(1)} %get-tuple-element.164), channel_id=1, source_target_pairs={{0,16},{16,32},{32,48},{48,64},{64,80},{80,96},{96,112},{112,128},... | collective-permute-start | bytes 786440 | tf_op jit(solution)/shard_map/while/body/eval_jaxpr/ppermute | solution.py:39
  379.4 12.7 %collective-permute-start = (f32[256,256]{1,0:T(8,128)S(1)}, f32[256,256]{1,0:T(8,128)S(1)}, u32[]{:S(2)}, u32[]{:S(2)}) collective-permute-start(f32[256,256]{1,0:T(8,128)S(1)} %get-tuple-element.164), channel_id=1, source_target_pairs={{0,16},{16,32},{32,48},{48,64},{64,80},{80,96},{96,112},{112,128},... | collective-permute-start | bytes 786440 | tf_op jit(solution)/shard_map/while/body/eval_jaxpr/ppermute | solution.py:39
  392.1 11.8 %collective-permute-start = (f32[256,256]{1,0:T(8,128)S(1)}, f32[256,256]{1,0:T(8,128)S(1)}, u32[]{:S(2)}, u32[]{:S(2)}) collective-permute-start(f32[256,256]{1,0:T(8,128)S(1)} %get-tuple-element.164), channel_id=1, source_target_pairs={{0,16},{16,32},{32,48},{48,64},{64,80},{80,96},{96,112},{112,128},... | collective-permute-start | bytes 786440 | tf_op jit(solution)/shard_map/while/body/eval_jaxpr/ppermute | solution.py:39
  403.9 11.6 %collective-permute-start = (f32[256,256]{1,0:T(8,128)S(1)}, f32[256,256]{1,0:T(8,128)S(1)}, u32[]{:S(2)}, u32[]{:S(2)}) collective-permute-start(f32[256,256]{1,0:T(8,128)S(1)} %get-tuple-element.164), channel_id=1, source_target_pairs={{0,16},{16,32},{32,48},{48,64},{64,80},{80,96},{96,112},{112,128},... | collective-permute-start | bytes 786440 | tf_op jit(solution)/shard_map/while/body/eval_jaxpr/ppermute | solution.py:39
  450.2 12.0 %collective-permute-start = (f32[256,256]{1,0:T(8,128)S(1)}, f32[256,256]{1,0:T(8,128)S(1)}, u32[]{:S(2)}, u32[]{:S(2)}) collective-permute-start(f32[256,256]{1,0:T(8,128)S(1)} %get-tuple-element.164), channel_id=1, source_target_pairs={{0,16},{16,32},{32,48},{48,64},{64,80},{80,96},{96,112},{112,128},... | collective-permute-start | bytes 786440 | tf_op jit(solution)/shard_map/while/body/eval_jaxpr/ppermute | solution.py:39
  485.4 11.6 %collective-permute-start = (f32[256,256]{1,0:T(8,128)S(1)}, f32[256,256]{1,0:T(8,128)S(1)}, u32[]{:S(2)}, u32[]{:S(2)}) collective-permute-start(f32[256,256]{1,0:T(8,128)S(1)} %get-tuple-element.164), channel_id=1, source_target_pairs={{0,16},{16,32},{32,48},{48,64},{64,80},{80,96},{96,112},{112,128},... | collective-permute-start | bytes 786440 | tf_op jit(solution)/shard_map/while/body/eval_jaxpr/ppermute | solution.py:39
  (26 other events, 233.9 us)
Sparse Core Ops, SparseCore 0:
  10.9 46.2 all-gather.1
